TPU v7x, 128 devices: a whole 4x4x4 slice. The times are simulated.
128 devices in a mesh: blk: 16 (over y, z), rep: 8 (over x, core).
Axes of the slice: x: 4, y: 4, z: 4, core: 2. Of those that a mesh axis runs over, the one named last changes fastest.
Arguments:
- dense: bfloat16 [131072, 1024], P(('blk', 'rep')), may hold values from -6 to 6
- labels: int32 [131072], P(('blk', 'rep')), may hold values 0 or 1
- tile_values: bfloat16 [16384, 64, 128], P(('blk', 'rep')), may hold values from -1.1953125 to 1.1953125
- tile_block: int32 [16384, 64], P(('blk', 'rep')), may hold values from 0 to 1023
- tile_example: int32 [16384, 64], P(('blk', 'rep')), may hold values from 0 to 1023
- tile_count: int32 [16384], P(('blk', 'rep')), may hold values from 16 to 64, as said below
- z_state: float32 [131072, 128], P(('blk', 'rep')), may hold values from -6 to 6
- n_state: float32 [131072, 128], P(('blk', 'rep')), may hold values from 0.01 to 4
- w_one: bfloat16 [1024, 512], replicated, may hold values from -0.1875 to 0.1875
- b_one: float32 [512], replicated, may hold values from -3 to 3
- w_two: bfloat16 [512, 256], replicated, may hold values from -0.25 to 0.25
- b_two: float32 [256], replicated, may hold values from -3 to 3
- head: bfloat16 [256], replicated, may hold values from -0.375 to 0.375
Outputs:
- probability: float32 [131072], P(('blk', 'rep'))
- z_new: float32 [131072, 128], P(('blk', 'rep'))
- n_new: float32 [131072, 128], P(('blk', 'rep'))
- grad_w_one: float32 [1024, 512], replicated
- grad_b_one: float32 [512], replicated
- grad_w_two: float32 [512, 256], replicated
- grad_b_two: float32 [256], replicated
- grad_head: float32 [256], replicated
Inputs may be any that keep to these rules, and one draw needn't show every extreme that they name: `tile_count`: slots at or beyond a list's count are padding; in every draw some owners receive 64 live slots from every device.
All inputs are finite; a program needn't handle non-finite values. No bound on the sum of `labels` on one device may be relied on, other than what follows from the above.
Results may differ from a plain program's by a relative error of at most 0.013.
Values may be sent and summed in bfloat16 or wider, within the bound.
A program may use at most 64 MiB of HBM per device.

v0:
```python
import jax
import jax.numpy as jnp
from jax import lax
from jax.sharding import PartitionSpec as P

alpha_rate = 0.5
beta_shift = 1.0
lasso_term = 0.5
ridge_term = 0.1


def wide_weight(z_state, n_state):
    shrunk = z_state - jnp.sign(z_state) * lasso_term
    denominator = (beta_shift + jnp.sqrt(n_state)) / alpha_rate + ridge_term
    return jnp.where(jnp.abs(z_state) > lasso_term, -shrunk / denominator, jnp.zeros_like(z_state))


def silu_slope(pre):
    gate = jax.nn.sigmoid(pre)
    return gate * (1.0 + pre * (1.0 - gate))


def per_device(
    dense,
    labels,
    tile_values,
    tile_block,
    tile_example,
    tile_count,
    z_state,
    n_state,
    w_one,
    b_one,
    w_two,
    b_two,
    head,
):
    owners, capacity, width = tile_values.shape
    slots = jnp.arange(capacity, dtype=jnp.int32)
    live = slots[None, :] < tile_count[:, None]
    masked = jnp.where(live[:, :, None], tile_values, jnp.zeros_like(tile_values))
    got_values, got_block = (
        lax.all_to_all(masked, ("blk", "rep"), split_axis=0, concat_axis=0, tiled=True),
        lax.all_to_all(tile_block, ("blk", "rep"), split_axis=0, concat_axis=0, tiled=True),
    )
    weight = wide_weight(z_state, n_state)
    flat_block = got_block.reshape(-1)
    flat_values = got_values.reshape(-1, width)
    picked = jnp.take(weight, flat_block, axis=0)
    tile_logit = jnp.sum(flat_values.astype(jnp.float32) * picked, axis=1).reshape(owners, capacity)
    returned = lax.all_to_all(tile_logit, ("blk", "rep"), split_axis=0, concat_axis=0, tiled=True)
    flat_example = tile_example.reshape(-1)
    wide = jnp.zeros((dense.shape[0],), jnp.float32).at[flat_example].add(returned.reshape(-1))
    pre_one = jnp.dot(dense, w_one, preferred_element_type=jnp.float32) + b_one
    hid_one = jax.nn.silu(pre_one).astype(jnp.bfloat16)
    pre_two = jnp.dot(hid_one, w_two, preferred_element_type=jnp.float32) + b_two
    hid_two = jax.nn.silu(pre_two).astype(jnp.bfloat16)
    deep = jnp.dot(hid_two, head, preferred_element_type=jnp.float32)
    probability = jax.nn.sigmoid(wide + deep)
    residual = probability - labels.astype(jnp.float32)
    tile_residual = jnp.take(residual, flat_example).reshape(owners, capacity)
    got_residual = lax.all_to_all(
        tile_residual, ("blk", "rep"), split_axis=0, concat_axis=0, tiled=True
    )
    contrib = flat_values.astype(jnp.float32) * got_residual.reshape(-1)[:, None]
    grad_block = jnp.zeros_like(z_state).at[flat_block].add(contrib)
    n_new = n_state + grad_block * grad_block
    sigma = (jnp.sqrt(n_new) - jnp.sqrt(n_state)) / alpha_rate
    z_new = z_state + grad_block - sigma * weight
    dlogit = residual.astype(jnp.bfloat16)
    grad_head = jnp.dot(dlogit, hid_two, preferred_element_type=jnp.float32)
    d_two = (
        dlogit.astype(jnp.float32)[:, None]
        * head.astype(jnp.float32)[None, :]
        * silu_slope(pre_two)
    ).astype(jnp.bfloat16)
    grad_w_two = lax.dot_general(
        hid_one, d_two, (((0,), (0,)), ((), ())), preferred_element_type=jnp.float32
    )
    grad_b_two = jnp.sum(d_two.astype(jnp.float32), axis=0)
    back_one = lax.dot_general(
        d_two, w_two, (((1,), (1,)), ((), ())), preferred_element_type=jnp.float32
    )
    d_one = (back_one * silu_slope(pre_one)).astype(jnp.bfloat16)
    grad_w_one = lax.dot_general(
        dense, d_one, (((0,), (0,)), ((), ())), preferred_element_type=jnp.float32
    )
    grad_b_one = jnp.sum(d_one.astype(jnp.float32), axis=0)
    grad_head, grad_w_two, grad_b_two, grad_w_one, grad_b_one = lax.psum(
        (grad_head, grad_w_two, grad_b_two, grad_w_one, grad_b_one), ("blk", "rep")
    )
    return (probability, z_new, n_new, grad_w_one, grad_b_one, grad_w_two, grad_b_two, grad_head)


def solution(mesh):
    placed = (
        P(("blk", "rep"), None),
        P(("blk", "rep")),
        P(("blk", "rep"), None, None),
        P(("blk", "rep"), None),
        P(("blk", "rep"), None),
        P(("blk", "rep")),
        P(("blk", "rep"), None),
        P(("blk", "rep"), None),
        P(),
        P(),
        P(),
        P(),
        P(),
    )
    return jax.shard_map(
        per_device,
        mesh=mesh,
        in_specs=placed,
        out_specs=(
            P(("blk", "rep")),
            P(("blk", "rep"), None),
            P(("blk", "rep"), None),
            P(),
            P(),
            P(),
            P(),
            P(),
        ),
        check_vma=False,
    )
```

profile of v0, /device:TPU:1, one launch (start us, length us, event | category | flops | bytes accessed | tf_op | source)
XLA Modules:
  0.0 373.5 jit_solution(6273867925865264041)
XLA Ops:
  7.2 1.6 copy.30
  8.8 11.5 %all-to-all-start.1 = ((s32[128,1,64]{2,1,0:T(1,128)}), s32[128,1,64]{2,1,0:T(1,128)S(1)}, u32[]{:S(2)}, u32[]{:S(2)}) async-start(s32[128,1,64]{2,1,0:T(1,128)} %bitcast.2), calls=%async_computation.1 | async-start | bytes 131072 | tf_op jit(solution)/shard_map/all_to_all | solution.py:44
  20.3 0.7 iota_compare_fusion
  21.1 0.7 reshape.183
  21.7 0.8 copy.29
  22.7 1.6 divide_select_fusion
  24.4 4.5 %broadcast_select_fusion = bf16[128,64,128]{2,1,0:T(8,128)(2,1)} fusion(bf16[128,64,128]{2,1,0:T(8,128)(2,1)} %param.15, pred[128,64]{1,0:T(8,128)(4,1)S(1)} %iota_compare_fusion), kind=kLoop, calls=%fused_computation.10 | loop fusion | flops 1048576 | bytes 4202496 | tf_op jit(solution)/shard_map/jit(_where)/select_n | solution.py:41
  29.0 2.8 multiply_convert_fusion.1
  31.7 1.4 multiply_convert_fusion.3
  33.4 10.2 %all-to-all-start = ((bf16[128,64,128]{2,1,0:T(8,128)(2,1)}), bf16[128,64,128]{2,1,0:T(8,128)(2,1)}, u32[]{:S(2)}, u32[]{:S(2)}) async-start(bf16[128,64,128]{2,1,0:T(8,128)(2,1)} %broadcast_select_fusion), calls=%async_computation | async-start | bytes 4194304 | tf_op jit(solution)/shard_map/all_to_all | solution.py:43
  44.1 0.8 reduce.10
  45.1 27.8 %gather_fusion = f32[8192,128]{1,0:T(8,128)} fusion(f32[1024,128]{1,0:T(8,128)S(1)} %divide_select_fusion, s32[8192]{0:T(1024)S(1)} %broadcast_clamp_fusion.1), kind=kCustom, calls=%fused_computation | custom fusion | bytes 8421376 | tf_op jit(solution)/shard_map/jit(_take)/gather | solution.py:49
  72.9 0.9 all-to-all-done
  73.8 5.4 %multiply_reduce_fusion = f32[128,64]{1,0:T(8,128)} fusion(f32[128,64,128]{2,1,0:T(8,128)} %bitcast.30, pred[128,64]{1,0:T(8,128)(4,1)S(1)} %compare_and_fusion, bf16[128,64,128]{2,1,0:T(8,128)(2,1)} %all-to-all-done), kind=kLoop, calls=%fused_computation.5 | loop fusion | flops 4186112 | bytes 6332416 | tf_op jit(solution)/shard_map/reduce_sum | solution.py:50
  79.2 8.9 %all-to-all-start.2 = ((f32[128,1,64]{2,1,0:T(1,128)}), f32[128,1,64]{2,1,0:T(1,128)S(1)}, u32[]{:S(2)}, u32[]{:S(2)}) async-start(f32[128,1,64]{2,1,0:T(1,128)} %bitcast.6), calls=%async_computation.2 | async-start | bytes 131072 | tf_op jit(solution)/shard_map/all_to_all | solution.py:51
  88.2 9.4 %all-to-all-done.2 = f32[128,1,64]{2,1,0:T(1,128)S(1)} async-done(((f32[128,1,64]{2,1,0:T(1,128)}), f32[128,1,64]{2,1,0:T(1,128)S(1)}, u32[]{:S(2)}, u32[]{:S(2)}) %all-to-all-start.2) | async-done | bytes 32800 | tf_op jit(solution)/shard_map/all_to_all | solution.py:51
  98.0 0.8 reduce.11
  98.9 57.0 %scatter_fusion = f32[1024]{0:T(1024)S(1)} fusion(f32[1024]{0:T(1024)S(1)} %bitcast.29, s32[8192]{0:T(1024)S(1)} %bitcast.33, f32[8192]{0:T(1024)S(1)} %reshape.171), kind=kCustom, calls=%fused_computation.2 | custom fusion | flops 8192 | bytes 131072 | tf_op jit(solution)/shard_map/scatter-add | solution.py:53
  156.6 1.8 convert_reduce_fusion.1
  158.3 2.5 fusion.4
  160.8 1.0 convert_reduce_fusion
  161.9 2.6 convolution_bitcast_fusion
  164.5 32.9 %gather_fusion.1 = f32[8192]{0:T(1024)S(1)} fusion(f32[1024]{0:T(1024)S(1)} %get-tuple-element.41, s32[8192]{0:T(1024)S(1)} %broadcast_clamp_fusion), kind=kCustom, calls=%fused_computation.1 | custom fusion | bytes 98304 | tf_op jit(solution)/shard_map/jit(_take)/gather | solution.py:61
  198.1 4.6 %all-to-all-start.3 = ((f32[128,1,64]{2,1,0:T(1,128)}), f32[128,1,64]{2,1,0:T(1,128)S(1)}, u32[]{:S(2)}, u32[]{:S(2)}) async-start(f32[128,1,64]{2,1,0:T(1,128)} %bitcast.9), calls=%async_computation.3 | async-start | bytes 131072 | tf_op jit(solution)/shard_map/all_to_all | solution.py:62
  203.4 67.4 %all-reduce = (f32[512]{0:T(512)}, f32[256]{0:T(256)}, f32[256]{0:T(256)}) all-reduce(f32[512]{0:T(512)S(1)} %get-tuple-element.49, f32[256]{0:T(256)S(1)} %get-tuple-element.37, f32[256]{0:T(256)S(1)} %bitcast.36), channel_id=1, replica_groups=mesh['blk'=16,'rep'=8] {'blk','rep'}, use_global_device_ids=true, to_apply=%region_5.6 | all-reduce | flops 1024 | bytes 8192 | tf_op jit(solution)/shard_map/psum | solution.py:89
  270.9 0.8 reduce.12
  271.8 3.9 %bitcast_multiply_fusion = f32[8192,128]{1,0:T(8,128)} fusion(f32[8192]{0:T(1024)S(1)} %mul.66, bf16[128,64,128]{2,1,0:T(8,128)(2,1)} %all-to-all-done), kind=kLoop, calls=%fused_computation.4 | loop fusion | flops 2097152 | bytes 6324224 | tf_op jit(solution)/shard_map/mul | solution.py:65
  275.7 45.1 %scatter_custom_fusion.1 = f32[1024,128]{1,0:T(8,128)} fusion(s32[8192]{0:T(1024)S(1)} %bitcast.35, f32[8192,128]{1,0:T(8,128)} %bitcast_multiply_fusion, f32[]{:T(128)} %constant.32.clone.1), kind=kCustom, calls=%fused_computation.21 | custom fusion | flops 1048576 | bytes 524800 | tf_op jit(solution)/shard_map/scatter-add | solution.py:66
  320.7 2.7 multiply_subtract_fusion
  323.4 39.5 %all-reduce.4.cloned.1.call-done = (f32[1024,512]{0,1:T(8,128)}, f32[512,256]{1,0:T(8,128)}) async-done(((f32[1024,512]{0,1:T(8,128)}, f32[512,256]{1,0:T(8,128)}), (f32[1024,512]{0,1:T(8,128)}, f32[512,256]{1,0:T(8,128)})) %all-reduce.4.cloned.1.call-update) | async-done | bytes 2621456 | tf_op jit(solution)/shard_map/psum | solution.py:89
  362.9 2.9 copy.35
  365.8 0.8 copy.39
  (48 shorter events, 3.9 us)
Async XLA Ops:
  7.2 21.8 %copy-start = (bf16[1024,1024]{1,0:T(8,128)(2,1)S(1)}, bf16[1024,1024]{1,0:T(8,128)(2,1)}, u32[]{:S(2)}) copy-start(bf16[1024,1024]{1,0:T(8,128)(2,1)} %param.13) | copy-start | bytes 6291460
  8.8 24.6 %all-to-all-start.1 = ((s32[128,1,64]{2,1,0:T(1,128)}), s32[128,1,64]{2,1,0:T(1,128)S(1)}, u32[]{:S(2)}, u32[]{:S(2)}) async-start(s32[128,1,64]{2,1,0:T(1,128)} %bitcast.2), calls=%async_computation.1 | async-start | bytes 131072 | tf_op jit(solution)/shard_map/all_to_all | solution.py:44
  24.4 4.6 %copy-start.5 = (bf16[1024,512]{1,0:T(8,128)(2,1)S(1)}, bf16[1024,512]{1,0:T(8,128)(2,1)}, u32[]{:S(2)}) copy-start(bf16[1024,512]{1,0:T(8,128)(2,1)} %param.21) | copy-start | bytes 3145732
  24.4 4.5 %copy-start.8 = (f32[512]{0:T(512)S(1)}, f32[512]{0:T(512)}, u32[]{:S(2)}) copy-start(f32[512]{0:T(512)} %param.22) | copy-start | bytes 6148
  28.9 2.8 copy-start.6
  28.9 2.8 copy-start.9
  31.7 1.4 copy-start.11
  33.4 40.4 %all-to-all-start = ((bf16[128,64,128]{2,1,0:T(8,128)(2,1)}), bf16[128,64,128]{2,1,0:T(8,128)(2,1)}, u32[]{:S(2)}, u32[]{:S(2)}) async-start(bf16[128,64,128]{2,1,0:T(8,128)(2,1)} %broadcast_select_fusion), calls=%async_computation | async-start | bytes 4194304 | tf_op jit(solution)/shard_map/all_to_all | solution.py:43
  73.8 14.3 %copy-start.10 = (bf16[256]{0:T(256)(128)(2,1)S(1)}, bf16[256]{0:T(256)(128)(2,1)}, u32[]{:S(2)}) copy-start(bf16[256]{0:T(256)(128)(2,1)} %param.25) | copy-start | bytes 1540
  79.2 18.3 %all-to-all-start.2 = ((f32[128,1,64]{2,1,0:T(1,128)}), f32[128,1,64]{2,1,0:T(1,128)S(1)}, u32[]{:S(2)}, u32[]{:S(2)}) async-start(f32[128,1,64]{2,1,0:T(1,128)} %bitcast.6), calls=%async_computation.2 | async-start | bytes 131072 | tf_op jit(solution)/shard_map/all_to_all | solution.py:51
  98.9 57.0 %copy-start.4 = (s32[1024]{0:T(1024)S(1)}, s32[1024]{0:T(1024)}, u32[]{:S(2)}) copy-start(s32[1024]{0:T(1024)} %param.14) | copy-start | bytes 12292
  156.0 4.9 %copy-start.7 = (bf16[512,256]{1,0:T(8,128)(2,1)S(1)}, bf16[512,256]{1,0:T(8,128)(2,1)}, u32[]{:S(2)}) copy-start(bf16[512,256]{1,0:T(8,128)(2,1)} %param.23) | copy-start | bytes 786436
  156.0 4.9 %copy-start.12 = (f32[1024,512]{1,0:T(8,128)S(1)}, f32[1024,512]{1,0:T(8,128)}, u32[]{:S(2)}) copy-start(f32[1024,512]{1,0:T(8,128)} %get-tuple-element.46) | copy-start | bytes 6291460
  198.1 72.8 %all-to-all-start.3 = ((f32[128,1,64]{2,1,0:T(1,128)}), f32[128,1,64]{2,1,0:T(1,128)S(1)}, u32[]{:S(2)}, u32[]{:S(2)}) async-start(f32[128,1,64]{2,1,0:T(1,128)} %bitcast.9), calls=%async_computation.3 | async-start | bytes 131072 | tf_op jit(solution)/shard_map/all_to_all | solution.py:62
  202.7 160.2 %all-reduce.4.cloned.1.call-start = ((), (), s32[]{:S(2)}) async-start(), calls=%async_computation.4 | async-start | bytes 5242880 | tf_op jit(solution)/shard_map/psum | solution.py:89
  271.8 49.0 %copy-start.1 = (f32[1024,128]{1,0:T(8,128)S(1)}, f32[1024,128]{1,0:T(8,128)}, u32[]{:S(2)}) copy-start(f32[1024,128]{1,0:T(8,128)} %param.19) | copy-start | bytes 1572868
  271.8 49.0 %copy-start.2 = (f32[1024,128]{1,0:T(8,128)S(1)}, f32[1024,128]{1,0:T(8,128)}, u32[]{:S(2)}) copy-start(f32[1024,128]{1,0:T(8,128)} %param.20) | copy-start | bytes 1572868
  362.9 2.9 copy-start.3
Sparse Core Ops, SparseCore 0:
  209.1 153.7 all-reduce.3
where the time goes:
time: 374 us; the launch traced here: 373 us
  other arithmetic  127 us (34%)
  local copies, waits for them, and re-layouts  69 us (18%)
  blocking collectives  67.4 us (18%)
  waiting for transfers between devices  50.3 us (13%)
  starting transfers between devices  35.3 us (9%)
  between operations  14.3 us (4%)
  matrix products  10.7 us (3%)
    psum x1, blocking collectives, per_device(): lax.psum((grad_head, grad_w_two, grad_b_two, grad_w_one, grad_b_one), ('b...  67.4 us
    scatter-add x1, other arithmetic, per_device(): jnp.zeros((dense.shape[0],), jnp.float32).at[flat_example]  57 us
    scatter-add x1, other arithmetic, per_device(): grad_block = jnp.zeros_like(z_state).at[flat_block].add(contrib)  45.1 us
    psum x1, waiting for transfers between devices, per_device(): lax.psum((grad_head, grad_w_two, grad_b_two, grad_w_one, grad_b_one), ('b...  39.5 us
    gather x2, local copies, waits for them, and re-layouts, per_device(): tile_residual = jnp.take(residual, flat_example).reshape(owners, capacity)  32.9 us
    gather x1, local copies, waits for them, and re-layouts, per_device(): picked = jnp.take(weight, flat_block, axis=0)  27.8 us
    all_to_all x1, starting transfers between devices, per_device(): lax.all_to_all(tile_block, ('blk', 'rep'), split_axis=0, concat_axis=0, t...  11.5 us
    all_to_all x1, starting transfers between devices, per_device(): lax.all_to_all(masked, ('blk', 'rep'), split_axis=0, concat_axis=0, tiled...  10.2 us
  transfers between devices with their start and end apart: 5, of which 3 were waited for; matrix products, arithmetic and copies ran while one was open for 25% of the time, Pallas kernels for 0%

commit v1 on v0

--- a/solution.py
+++ b/solution.py
@@ -87,7 +87,7 @@
     )
     grad_b_one = jnp.sum(d_one.astype(jnp.float32), axis=0)
     grad_head, grad_w_two, grad_b_two, grad_w_one, grad_b_one = lax.psum(
-        (grad_head, grad_w_two, grad_b_two, grad_w_one, grad_b_one), ("blk", "rep")
+        lax.psum((grad_head, grad_w_two, grad_b_two, grad_w_one, grad_b_one), "rep"), "blk"
     )
     return (probability, z_new, n_new, grad_w_one, grad_b_one, grad_w_two, grad_b_two, grad_head)
 

time: 374 us -> 356 us (0.952)
  the two profiles are of different devices: /device:TPU:1 before, /device:TPU:0 now
where the time goes in v1:
time: 356 us
  other arithmetic  125 us (35%)
  local copies, waits for them, and re-layouts  68.7 us (19%)
  blocking collectives  57.1 us (16%)
  waiting for transfers between devices  40.4 us (11%)
  starting transfers between devices  39 us (11%)
  between operations  14.3 us (4%)
  matrix products  10.9 us (3%)
    scatter-add x1, other arithmetic, per_device(): jnp.zeros((dense.shape[0],), jnp.float32).at[flat_example]  57 us
    scatter-add x1, other arithmetic, per_device(): grad_block = jnp.zeros_like(z_state).at[flat_block].add(contrib)  45.1 us
    psum x1, blocking collectives, per_device(): lax.psum(lax.psum((grad_head, grad_w_two, grad_b_two, grad_w_one, grad_b_...  42.1 us
    gather x2, local copies, waits for them, and re-layouts, per_device(): tile_residual = jnp.take(residual, flat_example).reshape(owners, capacity)  33 us
    psum x1, waiting for transfers between devices, per_device(): lax.psum((grad_head, grad_w_two, grad_b_two, grad_w_one, grad_b_one), 'rep')  30.7 us
    gather x1, local copies, waits for them, and re-layouts, per_device(): picked = jnp.take(weight, flat_block, axis=0)  27.8 us
    psum x1, blocking collectives, per_device(): lax.psum((grad_head, grad_w_two, grad_b_two, grad_w_one, grad_b_one), 'rep')  15 us
    all_to_all x1, starting transfers between devices, per_device(): lax.all_to_all(tile_block, ('blk', 'rep'), split_axis=0, concat_axis=0, t...  11.1 us
  transfers between devices with their start and end apart: 6, of which 3 were waited for; matrix products, arithmetic and copies ran while one was open for 36% of the time, Pallas kernels for 0%

profile of v1, /device:TPU:0, one launch (start us, length us, event | category | flops | bytes accessed | tf_op | source)
XLA Modules:
  0.0 355.6 jit_solution(14354165071060389675)
XLA Ops:
  7.2 1.6 copy.30
  8.8 11.1 %all-to-all-start.1 = ((s32[128,1,64]{2,1,0:T(1,128)}), s32[128,1,64]{2,1,0:T(1,128)S(1)}, u32[]{:S(2)}, u32[]{:S(2)}) async-start(s32[128,1,64]{2,1,0:T(1,128)} %bitcast.2), calls=%async_computation.1 | async-start | bytes 131072 | tf_op jit(solution)/shard_map/all_to_all | solution.py:44
  20.0 0.7 iota_compare_fusion
  20.7 0.8 copy.29
  21.7 4.5 %broadcast_select_fusion = bf16[128,64,128]{2,1,0:T(8,128)(2,1)} fusion(bf16[128,64,128]{2,1,0:T(8,128)(2,1)} %param.15, pred[128,64]{1,0:T(8,128)(4,1)S(1)} %iota_compare_fusion), kind=kLoop, calls=%fused_computation.10 | loop fusion | flops 1048576 | bytes 4202496 | tf_op jit(solution)/shard_map/jit(_where)/select_n | solution.py:41
  26.3 2.8 multiply_convert_fusion.1
  29.1 1.6 multiply_convert_fusion.3
  31.5 10.3 %all-to-all-start = ((bf16[128,64,128]{2,1,0:T(8,128)(2,1)}), bf16[128,64,128]{2,1,0:T(8,128)(2,1)}, u32[]{:S(2)}, u32[]{:S(2)}) async-start(bf16[128,64,128]{2,1,0:T(8,128)(2,1)} %broadcast_select_fusion), calls=%async_computation | async-start | bytes 4194304 | tf_op jit(solution)/shard_map/all_to_all | solution.py:43
  42.4 0.8 reduce.10
  43.3 27.8 %gather_fusion = f32[8192,128]{1,0:T(8,128)} fusion(f32[1024,128]{1,0:T(8,128)S(1)} %divide_select_fusion, s32[8192]{0:T(1024)S(1)} %broadcast_clamp_fusion.1), kind=kCustom, calls=%fused_computation | custom fusion | bytes 8421376 | tf_op jit(solution)/shard_map/jit(_take)/gather | solution.py:49
  71.1 0.7 all-to-all-done
  71.8 5.5 %multiply_reduce_fusion = f32[128,64]{1,0:T(8,128)} fusion(f32[128,64,128]{2,1,0:T(8,128)} %bitcast.30, pred[128,64]{1,0:T(8,128)(4,1)S(1)} %compare_and_fusion, bf16[128,64,128]{2,1,0:T(8,128)(2,1)} %all-to-all-done), kind=kLoop, calls=%fused_computation.5 | loop fusion | flops 4186112 | bytes 6332416 | tf_op jit(solution)/shard_map/reduce_sum | solution.py:50
  77.3 9.0 %all-to-all-start.2 = ((f32[128,1,64]{2,1,0:T(1,128)}), f32[128,1,64]{2,1,0:T(1,128)S(1)}, u32[]{:S(2)}, u32[]{:S(2)}) async-start(f32[128,1,64]{2,1,0:T(1,128)} %bitcast.6), calls=%async_computation.2 | async-start | bytes 131072 | tf_op jit(solution)/shard_map/all_to_all | solution.py:51
  86.6 8.9 %all-to-all-done.2 = f32[128,1,64]{2,1,0:T(1,128)S(1)} async-done(((f32[128,1,64]{2,1,0:T(1,128)}), f32[128,1,64]{2,1,0:T(1,128)S(1)}, u32[]{:S(2)}, u32[]{:S(2)}) %all-to-all-start.2) | async-done | bytes 32800 | tf_op jit(solution)/shard_map/all_to_all | solution.py:51
  96.1 0.8 reduce.11
  97.0 57.0 %scatter_fusion = f32[1024]{0:T(1024)S(1)} fusion(f32[1024]{0:T(1024)S(1)} %bitcast.29, s32[8192]{0:T(1024)S(1)} %bitcast.32, f32[8192]{0:T(1024)S(1)} %reshape.171), kind=kCustom, calls=%fused_computation.2 | custom fusion | flops 8192 | bytes 131072 | tf_op jit(solution)/shard_map/scatter-add | solution.py:53
  154.6 1.8 convert_reduce_fusion.1
  156.4 2.5 fusion.4
  158.9 1.0 convert_reduce_fusion
  159.9 2.6 convolution_bitcast_fusion
  162.6 32.9 %gather_fusion.1 = f32[8192]{0:T(1024)S(1)} fusion(f32[1024]{0:T(1024)S(1)} %get-tuple-element.46, s32[8192]{0:T(1024)S(1)} %broadcast_clamp_fusion), kind=kCustom, calls=%fused_computation.1 | custom fusion | bytes 98304 | tf_op jit(solution)/shard_map/jit(_take)/gather | solution.py:61
  195.6 30.7 %all-reduce.9.cloned.1.call-done = (f32[1024,512]{0,1:T(8,128)}, f32[512,256]{1,0:T(8,128)}) async-done(((f32[1024,512]{0,1:T(8,128)}, f32[512,256]{1,0:T(8,128)}), (f32[1024,512]{0,1:T(8,128)}, f32[512,256]{1,0:T(8,128)})) %all-reduce.9.cloned.1.call-update) | async-done | bytes 2621456 | tf_op jit(solution)/shard_map/psum | solution.py:90
  226.3 0.6 and_select_fusion
  226.9 8.4 %all-to-all-start.3 = ((f32[128,1,64]{2,1,0:T(1,128)}), f32[128,1,64]{2,1,0:T(1,128)S(1)}, u32[]{:S(2)}, u32[]{:S(2)}) async-start(f32[128,1,64]{2,1,0:T(1,128)} %bitcast.9), calls=%async_computation.3 | async-start | bytes 131072 | tf_op jit(solution)/shard_map/all_to_all | solution.py:62
  235.5 15.0 %all-reduce.2 = (f32[512]{0:T(512)S(1)}, f32[256]{0:T(256)S(1)}, f32[256]{0:T(256)S(1)}) all-reduce(f32[512]{0:T(512)S(1)} %get-tuple-element.54, f32[256]{0:T(256)S(1)} %get-tuple-element.42, f32[256]{0:T(256)S(1)} %bitcast.36), channel_id=1, replica_groups=mesh['blk'=16,'rep'=8] {'rep'}, use_global_device_ids=true, to_apply=%region_6.7 | all-reduce | flops 1024 | bytes 8192 | tf_op jit(solution)/shard_map/psum | solution.py:90
  250.5 42.1 %all-reduce = (f32[512]{0:T(512)}, f32[256]{0:T(256)}, f32[256]{0:T(256)}) all-reduce(f32[512]{0:T(512)S(1)} %get-tuple-element.37, f32[256]{0:T(256)S(1)} %get-tuple-element.38, f32[256]{0:T(256)S(1)} %get-tuple-element.39), channel_id=1, replica_groups=mesh['blk'=16,'rep'=8] {'blk'}, use_global_device_ids=true, to_apply=%region_7.8 | all-reduce | flops 1024 | bytes 8192 | tf_op jit(solution)/shard_map/psum | solution.py:89
  292.6 0.8 reduce.12
  293.5 3.8 %bitcast_multiply_fusion = f32[8192,128]{1,0:T(8,128)} fusion(f32[8192]{0:T(1024)S(1)} %mul.66, bf16[128,64,128]{2,1,0:T(8,128)(2,1)} %all-to-all-done), kind=kLoop, calls=%fused_computation.4 | loop fusion | flops 2097152 | bytes 6324224 | tf_op jit(solution)/shard_map/mul | solution.py:65
  297.3 45.1 %scatter_custom_fusion.1 = f32[1024,128]{1,0:T(8,128)} fusion(s32[8192]{0:T(1024)S(1)} %bitcast.35, f32[8192,128]{1,0:T(8,128)} %bitcast_multiply_fusion, f32[]{:T(128)} %constant.32.clone.1), kind=kCustom, calls=%fused_computation.21 | custom fusion | flops 1048576 | bytes 524800 | tf_op jit(solution)/shard_map/scatter-add | solution.py:66
  342.4 2.7 multiply_subtract_fusion
  345.1 2.9 copy.35
  348.0 0.8 copy.41
  (56 shorter events, 3.6 us)
Async XLA Ops:
  7.2 19.1 %copy-start = (bf16[1024,1024]{1,0:T(8,128)(2,1)S(1)}, bf16[1024,1024]{1,0:T(8,128)(2,1)}, u32[]{:S(2)}) copy-start(bf16[1024,1024]{1,0:T(8,128)(2,1)} %param.13) | copy-start | bytes 6291460
  8.8 22.7 %all-to-all-start.1 = ((s32[128,1,64]{2,1,0:T(1,128)}), s32[128,1,64]{2,1,0:T(1,128)S(1)}, u32[]{:S(2)}, u32[]{:S(2)}) async-start(s32[128,1,64]{2,1,0:T(1,128)} %bitcast.2), calls=%async_computation.1 | async-start | bytes 131072 | tf_op jit(solution)/shard_map/all_to_all | solution.py:44
  21.7 4.6 %copy-start.7 = (bf16[1024,512]{1,0:T(8,128)(2,1)S(1)}, bf16[1024,512]{1,0:T(8,128)(2,1)}, u32[]{:S(2)}) copy-start(bf16[1024,512]{1,0:T(8,128)(2,1)} %param.21) | copy-start | bytes 3145732
  21.7 4.6 %copy-start.10 = (f32[512]{0:T(512)S(1)}, f32[512]{0:T(512)}, u32[]{:S(2)}) copy-start(f32[512]{0:T(512)} %param.22) | copy-start | bytes 6148
  26.3 2.8 copy-start.8
  26.3 2.8 copy-start.11
  29.1 1.6 copy-start.13
  29.1 1.6 copy-start.1
  29.1 2.0 copy-start.2
  29.1 2.4 copy-start.12
  31.5 40.3 %all-to-all-start = ((bf16[128,64,128]{2,1,0:T(8,128)(2,1)}), bf16[128,64,128]{2,1,0:T(8,128)(2,1)}, u32[]{:S(2)}, u32[]{:S(2)}) async-start(bf16[128,64,128]{2,1,0:T(8,128)(2,1)} %broadcast_select_fusion), calls=%async_computation | async-start | bytes 4194304 | tf_op jit(solution)/shard_map/all_to_all | solution.py:43
  71.8 14.6 %copy-start.4 = (bf16[1024,256]{1,0:T(8,128)(2,1)S(1)}, bf16[1024,256]{1,0:T(8,128)(2,1)}, u32[]{:S(2)}) copy-start(bf16[1024,256]{1,0:T(8,128)(2,1)} %get-tuple-element.52) | copy-start | bytes 1572868
  77.3 18.3 %all-to-all-start.2 = ((f32[128,1,64]{2,1,0:T(1,128)}), f32[128,1,64]{2,1,0:T(1,128)S(1)}, u32[]{:S(2)}, u32[]{:S(2)}) async-start(f32[128,1,64]{2,1,0:T(1,128)} %bitcast.6), calls=%async_computation.2 | async-start | bytes 131072 | tf_op jit(solution)/shard_map/all_to_all | solution.py:51
  86.3 139.9 %all-reduce.9.cloned.1.call-start = ((), (), s32[]{:S(2)}) async-start(), calls=%async_computation.5 | async-start | bytes 5242880 | tf_op jit(solution)/shard_map/psum | solution.py:90
  97.0 57.0 %copy-start.6 = (s32[1024]{0:T(1024)S(1)}, s32[1024]{0:T(1024)}, u32[]{:S(2)}) copy-start(s32[1024]{0:T(1024)} %param.14) | copy-start | bytes 12292
  154.0 4.9 %copy-start.9 = (bf16[512,256]{1,0:T(8,128)(2,1)S(1)}, bf16[512,256]{1,0:T(8,128)(2,1)}, u32[]{:S(2)}) copy-start(bf16[512,256]{1,0:T(8,128)(2,1)} %param.23) | copy-start | bytes 786436
  154.0 4.9 %copy-start.14 = (f32[1024,512]{1,0:T(8,128)S(1)}, f32[1024,512]{1,0:T(8,128)}, u32[]{:S(2)}) copy-start(f32[1024,512]{1,0:T(8,128)} %get-tuple-element.51) | copy-start | bytes 6291460
  162.5 182.5 %all-reduce.7.cloned.1.call-start = ((), (), s32[]{:S(2)}) async-start(), calls=%async_computation.4 | async-start | bytes 5242880 | tf_op jit(solution)/shard_map/psum | solution.py:89
  226.9 65.7 %all-to-all-start.3 = ((f32[128,1,64]{2,1,0:T(1,128)}), f32[128,1,64]{2,1,0:T(1,128)S(1)}, u32[]{:S(2)}, u32[]{:S(2)}) async-start(f32[128,1,64]{2,1,0:T(1,128)} %bitcast.9), calls=%async_computation.3 | async-start | bytes 131072 | tf_op jit(solution)/shard_map/all_to_all | solution.py:62
  293.5 48.9 %copy-start.3 = (f32[1024,128]{1,0:T(8,128)S(1)}, f32[1024,128]{1,0:T(8,128)}, u32[]{:S(2)}) copy-start(f32[1024,128]{1,0:T(8,128)} %param.20) | copy-start | bytes 1572868
  345.1 2.9 copy-start.5
Sparse Core Ops, SparseCore 0:
  162.6 63.5 all-reduce.8
  229.7 92.9 all-reduce.6
